TPU v7x, 32 devices: a whole 2x2x4 slice. The times are simulated.
32 devices in a mesh: rows: 8 (over y, x, core), cols: 4 (over z).
Axes of the slice: x: 2, y: 2, z: 4, core: 2. Of those that a mesh axis runs over, the one named last changes fastest.
Arguments:
- grads: bfloat16 [2048, 4096], P('rows', 'cols'), may hold values from -6 to 6
- probe: bfloat16 [2048, 4096], P('rows', 'cols'), may hold values from -6 to 6
- left_factor: float32 [2048], P('rows'), may hold values from 0.5 to 2
- q_right: float32 [4096, 4096], P('cols', 'rows'), may hold values from -1 to 2
- q_inv_t: float32 [4096, 4096], P('cols', 'rows'), may hold values from -1 to 2
Outputs:
- left_new: float32 [2048], P('rows')
- q_new: float32 [4096, 4096], P('cols', 'rows')
All inputs are finite; a program needn't handle non-finite values. Where the computation divides by a largest or mean magnitude, that divisor is 1e-20 or more.
Results may differ from a plain program's by a relative error of at most 0.0058.
Values may be sent and summed in bfloat16 or wider, within the bound.
A program may use at most 64 MiB of HBM per device.

v0:
```python
import jax
import jax.numpy as jnp
from jax import lax
from jax.sharding import PartitionSpec as P


learn_rate = 0.2
epsilon = 1e-06


def shifted(x):
    cols = lax.axis_size("cols")
    return [x] + [
        lax.ppermute(x, "cols", [(c, (c + s) % cols) for c in range(cols)])
        for s in range(1, cols)
    ]


def after(x, earlier):
    return lax.optimization_barrier((x, earlier))[0]


def gather_halves(x):
    rows = lax.axis_size("rows")
    own = lax.all_gather(
        x, "rows", axis=0,
        axis_index_groups=[list(range(0, rows, 2)), list(range(1, rows, 2))],
    )
    return own, lax.ppermute(own, "rows", [(r, r ^ 1) for r in range(rows)])


def parities():
    core = lax.rem(lax.axis_index("rows"), 2)
    return core, 1 - core


def by_column(pieces):
    cols, rows = len(pieces), lax.axis_size("rows")
    me = lax.axis_index("cols")
    pairs = rows // cols // 2
    height, width = pieces[0].shape
    width = width * cols // rows
    halves = []
    for parity in parities():
        whole = jnp.zeros((rows // 2, height, width), pieces[0].dtype)
        for s, piece in enumerate(pieces):
            first = lax.rem(me - s + cols, cols) * pairs
            for t in range(pairs):
                block = lax.dynamic_slice_in_dim(piece, (2 * t + parity) * width, width, 1)
                whole = lax.dynamic_update_slice_in_dim(whole, block[None], first + t, 0)
        halves.append(whole)
    return halves


def dot_blocks(left, right, left_dims, right_dims):
    return lax.dot_general(
        left, right, ((left_dims, right_dims), ((), ())),
        preferred_element_type=jnp.float32,
    )


def body(grads, probe, left_factor, q_right, q_inv_t):
    rows = lax.axis_size("rows")

    def rotate(parts, factor_halves, gain):
        total = 0.0
        for x, f in zip(by_column(parts), factor_halves):
            total += dot_blocks(x, f, (0, 2), (0, 2))
        return (gain[:, None] * total).astype(jnp.bfloat16)

    probe_parts = shifted(probe)
    inv_halves = gather_halves(q_inv_t.astype(jnp.bfloat16))
    grad_parts = shifted(after(grads, probe_parts))
    q_low = q_right.astype(jnp.bfloat16)
    q_halves = gather_halves(q_low)
    conj_own = rotate(probe_parts, inv_halves, 1.0 / left_factor)
    conj_parts = shifted(conj_own)
    white_own = rotate(grad_parts, q_halves, left_factor)
    white_parts = shifted(white_own)
    q_parts = shifted(after(q_low, (conj_parts, white_parts)))
    conj_halves = gather_halves(conj_own)
    white_halves = gather_halves(white_own)

    def squares(parts):
        return sum(jnp.sum(jnp.square(p.astype(jnp.float32)), axis=1) for p in parts)

    left_grad = squares(white_parts) - squares(conj_parts)

    def pairs(parts, halves):
        own = lax.all_to_all(jnp.stack(parts), "rows", split_axis=2, concat_axis=1, tiled=True)
        own = own.reshape(own.shape[0], rows // 2, 2, -1, own.shape[2])
        total = 0.0
        for parity, half in zip(parities(), halves):
            mine = lax.dynamic_index_in_dim(own, parity, 2, keepdims=False)
            total += dot_blocks(mine, half, (1, 2), (0, 1))
        return total

    gram_block = pairs(conj_parts, conj_halves)
    gram_block = pairs(white_parts, white_halves) - gram_block
    gram_halves = gather_halves(gram_block.astype(jnp.bfloat16))
    top_r, top_l = lax.pmax(
        (jnp.max(jnp.abs(gram_block)), jnp.max(jnp.abs(left_grad))), ("rows", "cols")
    )
    scale_r = learn_rate / (top_r + epsilon)
    scale_l = learn_rate / (top_l + epsilon)
    left_new = left_factor - scale_l * left_grad * left_factor
    product = 0.0
    for parity, half in zip(parities(), gram_halves):
        blocks = [
            lax.dynamic_index_in_dim(
                p.reshape(rows // 2, 2, -1, p.shape[1]), parity, 1, keepdims=False
            )
            for p in q_parts
        ]
        product += dot_blocks(half, jnp.stack(blocks, axis=1), (0, 1, 2), (0, 1, 2))
    q_new = q_right - scale_r * product
    return (left_new, q_new)


def solution(mesh):
    return jax.shard_map(
        body,
        mesh=mesh,
        in_specs=(
            P("rows", "cols"),
            P("rows", "cols"),
            P("rows"),
            P("cols", "rows"),
            P("cols", "rows"),
        ),
        out_specs=(P("rows"), P("cols", "rows")),
        check_vma=False,
    )
```

profile of v0, /device:TPU:0, one launch (start us, length us, event | category | flops | bytes accessed | tf_op | source)
XLA Modules:
  0.0 551.8 jit_solution(2673765311910195993)
XLA Ops:
  7.2 2.9 convert_element_type.39
  10.2 1.1 convert_element_type.45
  11.4 54.2 %all-gather.11.cloned.1.call-done = bf16[4096,512]{1,0:T(8,128)(2,1)} async-done(((bf16[1024,512]{1,0:T(8,128)(2,1)}), bf16[4096,512]{1,0:T(8,128)(2,1)}) %all-gather.11.cloned.1.call-update) | async-done | bytes 4194320 | tf_op jit(solution)/shard_map/all_gather | solution.py:25
  65.6 1.5 collective-permute-start
  67.0 2.4 collective-permute-start.1
  69.5 1.4 collective-permute-start.2
  70.9 49.7 %all-gather.13.cloned.1.call-done = bf16[4096,512]{1,0:T(8,128)(2,1)} async-done(((bf16[1024,512]{1,0:T(8,128)(2,1)}), bf16[4096,512]{1,0:T(8,128)(2,1)}) %all-gather.13.cloned.1.call-update) | async-done | bytes 4194320 | tf_op jit(solution)/shard_map/all_gather | solution.py:25
  120.6 1.5 collective-permute-start.3
  122.1 2.4 collective-permute-start.4
  124.6 1.4 collective-permute-start.5
  126.2 11.3 %collective-permute-done.3 = bf16[256,1024]{1,0:T(8,128)(2,1)} collective-permute-done((bf16[256,1024]{1,0:T(8,128)(2,1)S(1)}, bf16[256,1024]{1,0:T(8,128)(2,1)}, u32[]{:S(2)}, u32[]{:S(2)}) %collective-permute-start.3) | collective-permute-done | bytes 524320 | tf_op jit(solution)/shard_map/ppermute | solution.py:14
  138.6 20.9 %collective-permute-done.4 = bf16[256,1024]{1,0:T(8,128)(2,1)} collective-permute-done((bf16[256,1024]{1,0:T(8,128)(2,1)S(1)}, bf16[256,1024]{1,0:T(8,128)(2,1)}, u32[]{:S(2)}, u32[]{:S(2)}) %collective-permute-start.4) | collective-permute-done | bytes 524320 | tf_op jit(solution)/shard_map/ppermute | solution.py:14
  159.5 1.1 bitcast_dynamic-update-slice_fusion.13
  160.6 3.6 convolution_bitcast_fusion.2
  164.3 2.1 multiply_reduce_fusion.7
  166.9 3.6 convolution_bitcast_fusion
  170.6 1.4 multiply_reduce_fusion.3
  172.0 12.7 %collective-permute-start.13 = (bf16[256,1024]{1,0:T(8,128)(2,1)S(1)}, bf16[256,1024]{1,0:T(8,128)(2,1)S(1)}, u32[]{:S(2)}, u32[]{:S(2)}) collective-permute-start(bf16[256,1024]{1,0:T(8,128)(2,1)S(1)} %get-tuple-element.33), channel_id=1, source_target_pairs={{0,3},{1,0},{2,1},{3,2},{4,7},{5,4},{6,5},{7,6},{8,11},{9,8},{10,9... | collective-permute-start | bytes 1572872 | tf_op jit(solution)/shard_map/ppermute | solution.py:14
  185.3 11.7 %collective-permute-done.13 = bf16[256,1024]{1,0:T(8,128)(2,1)S(1)} collective-permute-done((bf16[256,1024]{1,0:T(8,128)(2,1)S(1)}, bf16[256,1024]{1,0:T(8,128)(2,1)S(1)}, u32[]{:S(2)}, u32[]{:S(2)}) %collective-permute-start.13) | collective-permute-done | bytes 524320 | tf_op jit(solution)/shard_map/ppermute | solution.py:14
  197.0 32.6 %collective-permute-done.12 = bf16[256,1024]{1,0:T(8,128)(2,1)S(1)} collective-permute-done((bf16[256,1024]{1,0:T(8,128)(2,1)S(1)}, bf16[256,1024]{1,0:T(8,128)(2,1)S(1)}, u32[]{:S(2)}, u32[]{:S(2)}) %collective-permute-start.12) | collective-permute-done | bytes 524320 | tf_op jit(solution)/shard_map/ppermute | solution.py:14
  230.4 1.5 pad_maximum_fusion.1
  231.8 2.6 copy.28
  234.5 3.6 all-to-all-start.1
  238.1 2.4 collective-permute-start.8
  240.6 1.9 collective-permute-start.7
  242.5 10.0 %collective-permute-done.9 = bf16[256,1024]{1,0:T(8,128)(2,1)S(1)} collective-permute-done((bf16[256,1024]{1,0:T(8,128)(2,1)}, bf16[256,1024]{1,0:T(8,128)(2,1)S(1)}, u32[]{:S(2)}, u32[]{:S(2)}) %collective-permute-start.9) | collective-permute-done | bytes 524320 | tf_op jit(solution)/shard_map/ppermute | solution.py:14
  252.5 34.3 %collective-permute-done.8 = bf16[256,1024]{1,0:T(8,128)(2,1)S(1)} collective-permute-done((bf16[256,1024]{1,0:T(8,128)(2,1)}, bf16[256,1024]{1,0:T(8,128)(2,1)S(1)}, u32[]{:S(2)}, u32[]{:S(2)}) %collective-permute-start.8) | collective-permute-done | bytes 524320 | tf_op jit(solution)/shard_map/ppermute | solution.py:14
  287.8 2.6 pad_maximum_fusion
  290.5 4.3 copy.23
  294.8 4.4 all-to-all-start
  300.0 1.6 copy.29
  301.6 3.9 copy.30
  305.5 20.3 %all-to-all-done = bf16[4,256,1024]{1,0,2:T(4,128)(2,1)} async-done(((bf16[4,256,1024]{1,0,2:T(4,128)(2,1)}), bf16[4,256,1024]{1,0,2:T(4,128)(2,1)}, u32[]{:S(2)}, u32[]{:S(2)}) %all-to-all-start) | async-done | bytes 2097184 | tf_op jit(solution)/shard_map/all_to_all | solution.py:90
  325.8 1.9 copy.24
  327.6 2.4 copy.25
  330.0 3.3 fusion.34
  333.4 1.3 fusion.37
  334.7 3.0 fusion.21
  337.7 4.6 fusion.49
  342.4 49.1 %all-gather.19.cloned.1.call-done = bf16[16,128,1024]{2,1,0:T(8,128)(2,1)} async-done(((bf16[4,128,1024]{2,1,0:T(8,128)(2,1)}), bf16[16,128,1024]{2,1,0:T(8,128)(2,1)}) %all-gather.19.cloned.1.call-update) | async-done | bytes 4194320 | tf_op jit(solution)/shard_map/all_gather | solution.py:25
  391.5 6.4 %copy.33 = bf16[16,128,1024]{1,2,0:T(8,128)(2,1)} copy(bf16[16,128,1024]{2,1,0:T(8,128)(2,1)} %all-gather.19.cloned.1.call-done) | data formatting | bytes 8388608 | tf_op jit(solution)/shard_map/all_gather | solution.py:25
  397.9 3.4 collective-permute-start.18
  401.3 1.1 collective-permute-start.16
  404.4 20.5 %collective-permute-done.18 = bf16[1024,512]{1,0:T(8,128)(2,1)S(1)} collective-permute-done((bf16[1024,512]{1,0:T(8,128)(2,1)S(1)}, bf16[1024,512]{1,0:T(8,128)(2,1)S(1)}, u32[]{:S(2)}, u32[]{:S(2)}) %collective-permute-start.18) | collective-permute-done | bytes 1048608 | tf_op jit(solution)/shard_map/ppermute | solution.py:14
  425.8 66.0 %collective-permute-done.17 = bf16[1024,512]{1,0:T(8,128)(2,1)S(1)} collective-permute-done((bf16[1024,512]{1,0:T(8,128)(2,1)S(1)}, bf16[1024,512]{1,0:T(8,128)(2,1)S(1)}, u32[]{:S(2)}, u32[]{:S(2)}) %collective-permute-start.17) | collective-permute-done | bytes 1048608 | tf_op jit(solution)/shard_map/ppermute | solution.py:14
  493.6 38.9 %all-reduce = (f32[]{:T(128)}, f32[]{:T(128)}) all-reduce(f32[]{:T(128)} %get-tuple-element.8, f32[]{:T(128)} %get-tuple-element.11), channel_id=1, replica_groups=mesh['rows'=8,'cols'=4] {'rows','cols'}, use_global_device_ids=true, to_apply=%region_9.10 | all-reduce | flops 2 | bytes 16 | tf_op jit(solution)/shard_map/pmax | solution.py:101
  534.4 5.0 fusion
  539.4 5.9 %fusion.17 = f32[1024,512]{1,0:T(8,128)} fusion(f32[1024,512]{1,0:T(8,128)S(1)} %copy-done.4, f32[1024,512,1,1]{1,0,3,2:T(8,128)S(1)} %fusion, bf16[4,4,128,1024]{2,3,1,0:T(8,128)(2,1)} %collective-permute-done.19, bf16[4,1,128,512]{3,2,1,0:T(8,128)(2,1)S(1)} %get-tuple-element.18, bf16[4,1,128,512]{3,2,1,0:T(8,128)(2,1)S(1)} %get-tuple-element.16, ...), kind=kOutput, calls=%fused_computation.20 | convolution fusion | flops 2152202240 | bytes 12582916 | tf_op jit(solution)/shard_map/dot_general | solution.py:56
  (102 shorter events, 10.6 us)
Async XLA Ops:
  7.2 3.0 copy-start.3
  7.2 58.4 %all-gather.11.cloned.1.call-start = ((), (), s32[]{:S(2)}) async-start(), calls=%async_computation.2 | async-start | bytes 5242880 | tf_op jit(solution)/shard_map/all_gather | solution.py:25
  10.1 55.5 %copy-start.16 = (bf16[256,1024]{1,0:T(8,128)(2,1)S(1)}, bf16[256,1024]{1,0:T(8,128)(2,1)}, u32[]{:S(2)}) copy-start(bf16[256,1024]{1,0:T(8,128)(2,1)} %param.6) | copy-start | bytes 1572868
  10.1 110.5 %copy-start.15 = (bf16[256,1024]{1,0:T(8,128)(2,1)S(1)}, bf16[256,1024]{1,0:T(8,128)(2,1)}, u32[]{:S(2)}) copy-start(bf16[256,1024]{1,0:T(8,128)(2,1)} %param.5) | copy-start | bytes 1572868
  10.1 110.4 %all-gather.13.cloned.1.call-start = ((), (), s32[]{:S(2)}) async-start(), calls=%async_computation.3 | async-start | bytes 5242880 | tf_op jit(solution)/shard_map/all_gather | solution.py:25
  11.3 288.1 %all-gather.15.cloned.1.call-start = ((), (), s32[]{:S(2)}) async-start(), calls=%async_computation.4 | async-start | bytes 2621440 | tf_op jit(solution)/shard_map/all_gather | solution.py:25
  65.6 95.1 %collective-permute-start.6 = (bf16[4,1024,512]{2,1,0:T(8,128)(2,1)}, bf16[4,1024,512]{2,1,0:T(8,128)(2,1)}, u32[]{:S(2)}, u32[]{:S(2)}) collective-permute-start(bf16[4,1024,512]{2,1,0:T(8,128)(2,1)} %bitcast.176), channel_id=1, source_target_pairs={{0,4},{4,0},{8,12},{12,8},{16,20},{20,16},{24,28},{28,24},{1,5},{5... | collective-permute-start | bytes 12582920 | tf_op jit(solution)/shard_map/ppermute | solution.py:29
  65.6 55.0 %collective-permute-start = (bf16[256,1024]{1,0:T(8,128)(2,1)S(1)}, bf16[256,1024]{1,0:T(8,128)(2,1)S(1)}, u32[]{:S(2)}, u32[]{:S(2)}) collective-permute-start(bf16[256,1024]{1,0:T(8,128)(2,1)S(1)} %copy-done.16), channel_id=1, source_target_pairs={{0,1},{1,2},{2,3},{3,0},{4,5},{5,6},{6,7},{7,4},{8,9},{9,10},{10,1... | collective-permute-start | bytes 1572872 | tf_op jit(solution)/shard_map/ppermute | solution.py:14
  67.0 53.5 %collective-permute-start.1 = (bf16[256,1024]{1,0:T(8,128)(2,1)S(1)}, bf16[256,1024]{1,0:T(8,128)(2,1)S(1)}, u32[]{:S(2)}, u32[]{:S(2)}) collective-permute-start(bf16[256,1024]{1,0:T(8,128)(2,1)S(1)} %copy-done.16), channel_id=1, source_target_pairs={{0,2},{1,3},{2,0},{3,1},{4,6},{5,7},{6,4},{7,5},{8,10},{9,11},{10,... | collective-permute-start | bytes 1572872 | tf_op jit(solution)/shard_map/ppermute | solution.py:14
  69.5 51.1 %collective-permute-start.2 = (bf16[256,1024]{1,0:T(8,128)(2,1)S(1)}, bf16[256,1024]{1,0:T(8,128)(2,1)S(1)}, u32[]{:S(2)}, u32[]{:S(2)}) collective-permute-start(bf16[256,1024]{1,0:T(8,128)(2,1)S(1)} %copy-done.16), channel_id=1, source_target_pairs={{0,3},{1,0},{2,1},{3,2},{4,7},{5,4},{6,5},{7,6},{8,11},{9,8},{10,9... | collective-permute-start | bytes 1572872 | tf_op jit(solution)/shard_map/ppermute | solution.py:14
  120.6 46.3 %collective-permute-start.10 = (bf16[4,1024,512]{2,1,0:T(8,128)(2,1)}, bf16[4,1024,512]{2,1,0:T(8,128)(2,1)}, u32[]{:S(2)}, u32[]{:S(2)}) collective-permute-start(bf16[4,1024,512]{2,1,0:T(8,128)(2,1)} %bitcast.174), channel_id=1, source_target_pairs={{0,4},{4,0},{8,12},{12,8},{16,20},{20,16},{24,28},{28,24},{1,5},{5... | collective-permute-start | bytes 12582920 | tf_op jit(solution)/shard_map/ppermute | solution.py:29
  120.6 16.9 %collective-permute-start.3 = (bf16[256,1024]{1,0:T(8,128)(2,1)S(1)}, bf16[256,1024]{1,0:T(8,128)(2,1)}, u32[]{:S(2)}, u32[]{:S(2)}) collective-permute-start(bf16[256,1024]{1,0:T(8,128)(2,1)S(1)} %copy-done.15), channel_id=1, source_target_pairs={{0,1},{1,2},{2,3},{3,0},{4,5},{5,6},{6,7},{7,4},{8,9},{9,10},{10,1... | collective-permute-start | bytes 1572872 | tf_op jit(solution)/shard_map/ppermute | solution.py:14
  122.1 37.3 %collective-permute-start.4 = (bf16[256,1024]{1,0:T(8,128)(2,1)S(1)}, bf16[256,1024]{1,0:T(8,128)(2,1)}, u32[]{:S(2)}, u32[]{:S(2)}) collective-permute-start(bf16[256,1024]{1,0:T(8,128)(2,1)S(1)} %copy-done.15), channel_id=1, source_target_pairs={{0,2},{1,3},{2,0},{3,1},{4,6},{5,7},{6,4},{7,5},{8,10},{9,11},{10,... | collective-permute-start | bytes 1572872 | tf_op jit(solution)/shard_map/ppermute | solution.py:14
  124.6 36.0 %collective-permute-start.5 = (bf16[256,1024]{1,0:T(8,128)(2,1)S(1)}, bf16[256,1024]{1,0:T(8,128)(2,1)S(1)}, u32[]{:S(2)}, u32[]{:S(2)}) collective-permute-start(bf16[256,1024]{1,0:T(8,128)(2,1)S(1)} %copy-done.15), channel_id=1, source_target_pairs={{0,3},{1,0},{2,1},{3,2},{4,7},{5,4},{6,5},{7,6},{8,11},{9,8},{10,9... | collective-permute-start | bytes 1572872 | tf_op jit(solution)/shard_map/ppermute | solution.py:14
  160.6 3.7 copy-start.18
  160.6 3.7 copy-start.20
  166.4 133.2 %all-gather.17.cloned.1.call-start = ((), (), s32[]{:S(2)}) async-start(), calls=%async_computation.5 | async-start | bytes 2621440 | tf_op jit(solution)/shard_map/all_gather | solution.py:25
  166.9 3.6 copy-start.19
  172.0 13.3 %copy-start.14 = (bf16[256,1024]{1,0:T(8,128)(2,1)}, bf16[256,1024]{1,0:T(8,128)(2,1)S(1)}, u32[]{:S(2)}) copy-start(bf16[256,1024]{1,0:T(8,128)(2,1)S(1)} %get-tuple-element.33) | copy-start | bytes 1572868
  172.0 25.0 %collective-permute-start.13 = (bf16[256,1024]{1,0:T(8,128)(2,1)S(1)}, bf16[256,1024]{1,0:T(8,128)(2,1)S(1)}, u32[]{:S(2)}, u32[]{:S(2)}) collective-permute-start(bf16[256,1024]{1,0:T(8,128)(2,1)S(1)} %get-tuple-element.33), channel_id=1, source_target_pairs={{0,3},{1,0},{2,1},{3,2},{4,7},{5,4},{6,5},{7,6},{8,11},{9,8},{10,9... | collective-permute-start | bytes 1572872 | tf_op jit(solution)/shard_map/ppermute | solution.py:14
  184.7 44.9 %collective-permute-start.12 = (bf16[256,1024]{1,0:T(8,128)(2,1)S(1)}, bf16[256,1024]{1,0:T(8,128)(2,1)S(1)}, u32[]{:S(2)}, u32[]{:S(2)}) collective-permute-start(bf16[256,1024]{1,0:T(8,128)(2,1)S(1)} %get-tuple-element.33), channel_id=1, source_target_pairs={{0,2},{1,3},{2,0},{3,1},{4,6},{5,7},{6,4},{7,5},{8,10},{9,11},{10,... | collective-permute-start | bytes 1572872 | tf_op jit(solution)/shard_map/ppermute | solution.py:14
  184.7 44.9 %collective-permute-start.11 = (bf16[256,1024]{1,0:T(8,128)(2,1)S(1)}, bf16[256,1024]{1,0:T(8,128)(2,1)S(1)}, u32[]{:S(2)}, u32[]{:S(2)}) collective-permute-start(bf16[256,1024]{1,0:T(8,128)(2,1)S(1)} %get-tuple-element.33), channel_id=1, source_target_pairs={{0,1},{1,2},{2,3},{3,0},{4,5},{5,6},{6,7},{7,4},{8,9},{9,10},{10,1... | collective-permute-start | bytes 1572872 | tf_op jit(solution)/shard_map/ppermute | solution.py:14
  229.6 0.8 copy-start.6
  234.5 60.3 %all-to-all-start.1 = ((bf16[4,256,1024]{1,0,2:T(4,128)(2,1)}), bf16[4,256,1024]{1,0,2:T(4,128)(2,1)S(1)}, u32[]{:S(2)}, u32[]{:S(2)}) async-start(bf16[4,256,1024]{1,0,2:T(4,128)(2,1)} %copy.28), calls=%async_computation.1 | async-start | bytes 4194304 | tf_op jit(solution)/shard_map/all_to_all | solution.py:90
  238.1 14.4 %collective-permute-start.9 = (bf16[256,1024]{1,0:T(8,128)(2,1)}, bf16[256,1024]{1,0:T(8,128)(2,1)S(1)}, u32[]{:S(2)}, u32[]{:S(2)}) collective-permute-start(bf16[256,1024]{1,0:T(8,128)(2,1)} %get-tuple-element.35), channel_id=1, source_target_pairs={{0,3},{1,0},{2,1},{3,2},{4,7},{5,4},{6,5},{7,6},{8,11},{9,8},{10,9... | collective-permute-start | bytes 1572872 | tf_op jit(solution)/shard_map/ppermute | solution.py:14
  238.1 48.7 %collective-permute-start.8 = (bf16[256,1024]{1,0:T(8,128)(2,1)}, bf16[256,1024]{1,0:T(8,128)(2,1)S(1)}, u32[]{:S(2)}, u32[]{:S(2)}) collective-permute-start(bf16[256,1024]{1,0:T(8,128)(2,1)} %get-tuple-element.35), channel_id=1, source_target_pairs={{0,2},{1,3},{2,0},{3,1},{4,6},{5,7},{6,4},{7,5},{8,10},{9,11},{10,... | collective-permute-start | bytes 1572872 | tf_op jit(solution)/shard_map/ppermute | solution.py:14
  240.6 46.3 %collective-permute-start.7 = (bf16[256,1024]{1,0:T(8,128)(2,1)}, bf16[256,1024]{1,0:T(8,128)(2,1)S(1)}, u32[]{:S(2)}, u32[]{:S(2)}) collective-permute-start(bf16[256,1024]{1,0:T(8,128)(2,1)} %get-tuple-element.35), channel_id=1, source_target_pairs={{0,1},{1,2},{2,3},{3,0},{4,5},{5,6},{6,7},{7,4},{8,9},{9,10},{10,1... | collective-permute-start | bytes 1572872 | tf_op jit(solution)/shard_map/ppermute | solution.py:14
  252.5 34.4 %copy-start.8 = (bf16[256,1024]{1,0:T(8,128)(2,1)}, bf16[256,1024]{1,0:T(8,128)(2,1)S(1)}, u32[]{:S(2)}) copy-start(bf16[256,1024]{1,0:T(8,128)(2,1)S(1)} %collective-permute-done.9) | copy-start | bytes 1572868
  286.9 0.8 copy-start.10
  286.9 1.0 copy-start.12
  294.8 31.0 %all-to-all-start = ((bf16[4,256,1024]{1,0,2:T(4,128)(2,1)}), bf16[4,256,1024]{1,0,2:T(4,128)(2,1)}, u32[]{:S(2)}, u32[]{:S(2)}) async-start(bf16[4,256,1024]{1,0,2:T(4,128)(2,1)} %copy.23), calls=%async_computation | async-start | bytes 4194304 | tf_op jit(solution)/shard_map/all_to_all | solution.py:90
  299.1 92.3 %all-gather.19.cloned.1.call-start = ((), (), s32[]{:S(2)}) async-start(), calls=%async_computation.6 | async-start | bytes 5242880 | tf_op jit(solution)/shard_map/all_gather | solution.py:25
  299.4 35.3 %collective-permute-start.14 = (bf16[4,256,1024]{2,1,0:T(8,128)(2,1)}, bf16[4,256,1024]{2,1,0:T(8,128)(2,1)}, u32[]{:S(2)}, u32[]{:S(2)}) collective-permute-start(bf16[4,256,1024]{2,1,0:T(8,128)(2,1)} %bitcast.159), channel_id=1, source_target_pairs={{0,4},{4,0},{8,12},{12,8},{16,20},{20,16},{24,28},{28,24},{1,5},{5... | collective-permute-start | bytes 6291464 | tf_op jit(solution)/shard_map/ppermute | solution.py:29
  299.6 38.1 %collective-permute-start.15 = (bf16[4,256,1024]{2,1,0:T(8,128)(2,1)}, bf16[4,256,1024]{2,1,0:T(8,128)(2,1)}, u32[]{:S(2)}, u32[]{:S(2)}) collective-permute-start(bf16[4,256,1024]{2,1,0:T(8,128)(2,1)} %bitcast.161), channel_id=1, source_target_pairs={{0,4},{4,0},{8,12},{12,8},{16,20},{20,16},{24,28},{28,24},{1,5},{5... | collective-permute-start | bytes 6291464 | tf_op jit(solution)/shard_map/ppermute | solution.py:29
  330.0 3.3 copy-start.1
  330.0 3.3 copy-start.5
  334.7 3.1 copy-start.2
  342.4 55.5 %copy-start = (bf16[1024,512]{1,0:T(8,128)(2,1)S(1)}, bf16[1024,512]{1,0:T(8,128)(2,1)}, u32[]{:S(2)}) copy-start(bf16[1024,512]{1,0:T(8,128)(2,1)} %convert_element_type.39) | copy-start | bytes 3145732
  342.4 60.3 %copy-start.7 = (bf16[256,1024]{1,0:T(8,128)(2,1)S(1)}, bf16[256,1024]{1,0:T(8,128)(2,1)}, u32[]{:S(2)}) copy-start(bf16[256,1024]{1,0:T(8,128)(2,1)} %copy-done.6) | copy-start | bytes 1572868
  397.9 5.2 copy-start.9
  397.9 5.3 copy-start.11
  397.9 141.5 %collective-permute-start.19 = (bf16[4,4,128,1024]{2,3,1,0:T(8,128)(2,1)}, bf16[4,4,128,1024]{2,3,1,0:T(8,128)(2,1)}, u32[]{:S(2)}, u32[]{:S(2)}) collective-permute-start(bf16[4,4,128,1024]{2,3,1,0:T(8,128)(2,1)} %bitcast.158), channel_id=1, source_target_pairs={{0,4},{4,0},{8,12},{12,8},{16,20},{20,16},{24,28},{28,24},{1,5},{5... | collective-permute-start | bytes 12582920 | tf_op jit(solution)/shard_map/ppermute | solution.py:29
  397.9 27.0 %collective-permute-start.18 = (bf16[1024,512]{1,0:T(8,128)(2,1)S(1)}, bf16[1024,512]{1,0:T(8,128)(2,1)S(1)}, u32[]{:S(2)}, u32[]{:S(2)}) collective-permute-start(bf16[1024,512]{1,0:T(8,128)(2,1)S(1)} %copy-done), channel_id=1, source_target_pairs={{0,3},{1,0},{2,1},{3,2},{4,7},{5,4},{6,5},{7,6},{8,11},{9,8},{10,9... | collective-permute-start | bytes 3145736 | tf_op jit(solution)/shard_map/ppermute | solution.py:14
  401.3 90.5 %collective-permute-start.17 = (bf16[1024,512]{1,0:T(8,128)(2,1)S(1)}, bf16[1024,512]{1,0:T(8,128)(2,1)S(1)}, u32[]{:S(2)}, u32[]{:S(2)}) collective-permute-start(bf16[1024,512]{1,0:T(8,128)(2,1)S(1)} %copy-done), channel_id=1, source_target_pairs={{0,2},{1,3},{2,0},{3,1},{4,6},{5,7},{6,4},{7,5},{8,10},{9,11},{10,... | collective-permute-start | bytes 3145736 | tf_op jit(solution)/shard_map/ppermute | solution.py:14
  401.3 91.4 %collective-permute-start.16 = (bf16[1024,512]{1,0:T(8,128)(2,1)S(1)}, bf16[1024,512]{1,0:T(8,128)(2,1)S(1)}, u32[]{:S(2)}, u32[]{:S(2)}) collective-permute-start(bf16[1024,512]{1,0:T(8,128)(2,1)S(1)} %copy-done), channel_id=1, source_target_pairs={{0,1},{1,2},{2,3},{3,0},{4,5},{5,6},{6,7},{7,4},{8,9},{9,10},{10,1... | collective-permute-start | bytes 3145736 | tf_op jit(solution)/shard_map/ppermute | solution.py:14
  402.6 1.0 copy-start.13
  492.7 41.7 %copy-start.17 = (bf16[4,1,128,512]{3,2,1,0:T(8,128)(2,1)S(1)}, bf16[4,1,128,512]{3,2,1,0:T(8,128)(2,1)}, u32[]{:S(2)}) copy-start(bf16[4,1,128,512]{3,2,1,0:T(8,128)(2,1)} %get-tuple-element.17) | copy-start | bytes 1572868
  534.4 5.0 copy-start.4
Sparse Core Ops, SparseCore 0:
  10.2 55.2 all-gather.10
  68.0 52.5 all-gather.12
  166.6 44.4 all-gather.14
  212.8 47.2 all-gather.16
  342.5 48.9 all-gather.18
where the time goes:
time: 553 us; the launch traced here: 552 us
  waiting for transfers between devices  381 us (69%)
  starting transfers between devices  41.9 us (8%)
  blocking collectives  38.9 us (7%)
  matrix products  33.9 us (6%)
  local copies, waits for them, and re-layouts  30.6 us (6%)
  between operations  15.5 us (3%)
  other arithmetic  10.3 us (2%)
    ppermute x15, waiting for transfers between devices, shifted(): lax.ppermute(x, 'cols', [(c, (c + s) % cols) for c in range(cols)])  207 us
    all_gather x5, waiting for transfers between devices, gather_halves(): lax.all_gather(x, 'rows', axis=0, axis_index_groups=[list(range(0, rows,...  153 us
    pmax x1, blocking collectives, body(): lax.pmax((jnp.max(jnp.abs(gram_block)), jnp.max(jnp.abs(left_grad))), ('r...  38.9 us
    dot_general x10, matrix products, dot_blocks(): lax.dot_general(left, right, ((left_dims, right_dims), ((), ())), preferr...  33.9 us
    ppermute x15, starting transfers between devices, shifted(): lax.ppermute(x, 'cols', [(c, (c + s) % cols) for c in range(cols)])  33 us
    all_to_all x2, waiting for transfers between devices, pairs(): lax.all_to_all(jnp.stack(parts), 'rows', split_axis=2, concat_axis=1, til...  20.3 us
  transfers between devices with their start and end apart: 27, of which 12 were waited for; matrix products, arithmetic and copies ran while one was open for 10% of the time, Pallas kernels for 0%

commit v1 on v0

--- a/solution.py
+++ b/solution.py
@@ -22,10 +22,13 @@
 
 def gather_halves(x):
     rows = lax.axis_size("rows")
-    own = lax.all_gather(
-        x, "rows", axis=0,
-        axis_index_groups=[list(range(0, rows, 2)), list(range(1, rows, 2))],
-    )
+    pair = lax.axis_index("rows") // 2
+    own = jnp.zeros((rows // 2, *x.shape), x.dtype)
+    for d in range(rows // 2):
+        part = x
+        if d > 0:
+            part = lax.ppermute(x, "rows", [(r, r ^ (2 * d)) for r in range(rows)])
+        own = lax.dynamic_update_slice_in_dim(own, part[None], lax.bitwise_xor(pair, d), 0)
     return own, lax.ppermute(own, "rows", [(r, r ^ 1) for r in range(rows)])
 
 
@@ -72,10 +75,11 @@
     inv_halves = gather_halves(q_inv_t.astype(jnp.bfloat16))
     grad_parts = shifted(after(grads, probe_parts))
     q_low = q_right.astype(jnp.bfloat16)
-    q_halves = gather_halves(q_low)
+    q_halves = gather_halves(after(q_low, inv_halves[0]))
     conj_own = rotate(probe_parts, inv_halves, 1.0 / left_factor)
     conj_parts = shifted(conj_own)
     white_own = rotate(grad_parts, q_halves, left_factor)
+    conj_parts = after(conj_parts, white_own)
     white_parts = shifted(white_own)
     q_parts = shifted(after(q_low, (conj_parts, white_parts)))
     conj_halves = gather_halves(conj_own)

time: 553 us -> 580 us (1.049)
  starting transfers between devices: 41.9 us -> 89.6 us
  waiting for transfers between devices: 381 us -> 336 us
  local copies, waits for them, and re-layouts: 30.6 us -> 62.2 us
  between operations: 15.5 us -> 2.44 us
  matrix products: 33.9 us -> 40.7 us
    all_gather x5 -> x0, waiting for transfers between devices: 153 us -> none  [gather_halves(): lax.all_gather(x, 'rows', axis=0, axis_index_groups=[list(range(0, rows,...]
    ppermute x0 -> x15, waiting for transfers between devices: none -> 138 us  [gather_halves(): part = lax.ppermute(x, 'rows', [(r, r ^ 2 * d) for r in range(rows)])]
    ppermute x15, starting transfers between devices: 33 us -> 64.1 us  [shifted(): lax.ppermute(x, 'cols', [(c, (c + s) % cols) for c in range(cols)])]
    dynamic_update_slice x0 -> x18, local copies, waits for them, and re-layouts: none -> 23.4 us  [gather_halves(): lax.dynamic_update_slice_in_dim(own, part[None], lax.bitwise_xor(pair, d)...]
    ppermute x15, waiting for transfers between devices: 207 us -> 186 us  [shifted(): lax.ppermute(x, 'cols', [(c, (c + s) % cols) for c in range(cols)])]
    ppermute x0 -> x15, starting transfers between devices: none -> 17.2 us  [gather_halves(): part = lax.ppermute(x, 'rows', [(r, r ^ 2 * d) for r in range(rows)])]
    broadcast_in_dim x0 -> x5, local copies, waits for them, and re-layouts: none -> 7.93 us  [the longest x4 7.13 us: gather_halves(): part[None]]
    all_to_all x2, waiting for transfers between devices: 20.3 us -> 12.8 us  [pairs(): lax.all_to_all(jnp.stack(parts), 'rows', split_axis=2, concat_axis=1, til...]
  transfers between devices with their start and end apart: 27 -> 37, of which waited for: 12 -> 18; matrix products, arithmetic and copies ran while one was open for 10% -> 15% of each run, Pallas kernels for 0% -> 0%
where the time goes in v1:
time: 580 us; the launch traced here: 579 us
  waiting for transfers between devices  336 us (58%)
  starting transfers between devices  89.6 us (15%)
  local copies, waits for them, and re-layouts  62.2 us (11%)
  matrix products  40.7 us (7%)
  blocking collectives  39.4 us (7%)
  other arithmetic  7.96 us (1%)
    ppermute x15, waiting for transfers between devices, shifted(): lax.ppermute(x, 'cols', [(c, (c + s) % cols) for c in range(cols)])  186 us
    ppermute x15, waiting for transfers between devices, gather_halves(): part = lax.ppermute(x, 'rows', [(r, r ^ 2 * d) for r in range(rows)])  138 us
    ppermute x15, starting transfers between devices, shifted(): lax.ppermute(x, 'cols', [(c, (c + s) % cols) for c in range(cols)])  64.1 us
    dot_general x10, matrix products, dot_blocks(): lax.dot_general(left, right, ((left_dims, right_dims), ((), ())), preferr...  40.7 us
    pmax x1, blocking collectives, body(): lax.pmax((jnp.max(jnp.abs(gram_block)), jnp.max(jnp.abs(left_grad))), ('r...  39.4 us
    dynamic_update_slice x18, local copies, waits for them, and re-layouts, gather_halves(): lax.dynamic_update_slice_in_dim(own, part[None], lax.bitwise_xor(pair, d)...  23.4 us
    ppermute x15, starting transfers between devices, gather_halves(): part = lax.ppermute(x, 'rows', [(r, r ^ 2 * d) for r in range(rows)])  17.2 us
    all_to_all x2, waiting for transfers between devices, pairs(): lax.all_to_all(jnp.stack(parts), 'rows', split_axis=2, concat_axis=1, til...  12.8 us
  transfers between devices with their start and end apart: 37, of which 18 were waited for; matrix products, arithmetic and copies ran while one was open for 15% of the time, Pallas kernels for 0%

profile of v1, /device:TPU:0, one launch (start us, length us, event | category | flops | bytes accessed | tf_op | source)
XLA Modules:
  0.0 578.8 jit_solution(15542444370526466258)
XLA Ops:
  0.7 2.4 broadcast.17.clone
  4.5 3.0 collective-permute-start.6
  9.2 22.6 %collective-permute-done.6 = bf16[1024,512]{1,0:T(8,128)(2,1)} collective-permute-done((bf16[1024,512]{1,0:T(8,128)(2,1)}, bf16[1024,512]{1,0:T(8,128)(2,1)}, u32[]{:S(2)}, u32[]{:S(2)}) %collective-permute-start.6) | collective-permute-done | bytes 1048608 | tf_op jit(solution)/shard_map/ppermute | solution.py:30
  31.8 2.3 bitcast_dynamic-update-slice_fusion.6
  34.1 20.8 %collective-permute-done.7 = bf16[1024,512]{1,0:T(8,128)(2,1)} collective-permute-done((bf16[1024,512]{1,0:T(8,128)(2,1)}, bf16[1024,512]{1,0:T(8,128)(2,1)}, u32[]{:S(2)}, u32[]{:S(2)}) %collective-permute-start.7) | collective-permute-done | bytes 1048608 | tf_op jit(solution)/shard_map/ppermute | solution.py:30
  54.9 2.2 bitcast_dynamic-update-slice_fusion.5
  57.1 2.3 bitcast_dynamic-update-slice_fusion.4
  63.0 2.3 broadcast.17
  66.3 19.2 %collective-permute-done.9 = bf16[1024,512]{1,0:T(8,128)(2,1)S(1)} collective-permute-done((bf16[1024,512]{1,0:T(8,128)(2,1)S(1)}, bf16[1024,512]{1,0:T(8,128)(2,1)S(1)}, u32[]{:S(2)}, u32[]{:S(2)}) %collective-permute-start.9) | collective-permute-done | bytes 1048608 | tf_op jit(solution)/shard_map/ppermute | solution.py:30
  86.5 18.2 %collective-permute-done.10 = bf16[1024,512]{1,0:T(8,128)(2,1)S(1)} collective-permute-done((bf16[1024,512]{1,0:T(8,128)(2,1)S(1)}, bf16[1024,512]{1,0:T(8,128)(2,1)S(1)}, u32[]{:S(2)}, u32[]{:S(2)}) %collective-permute-start.10) | collective-permute-done | bytes 1048608 | tf_op jit(solution)/shard_map/ppermute | solution.py:30
  108.4 2.6 collective-permute-start.1
  112.6 12.0 %collective-permute-done = bf16[256,1024]{1,0:T(8,128)(2,1)} collective-permute-done((bf16[256,1024]{1,0:T(8,128)(2,1)S(1)}, bf16[256,1024]{1,0:T(8,128)(2,1)}, u32[]{:S(2)}, u32[]{:S(2)}) %collective-permute-start) | collective-permute-done | bytes 524320 | tf_op jit(solution)/shard_map/ppermute | solution.py:14
  124.6 21.8 %collective-permute-done.1 = bf16[256,1024]{1,0:T(8,128)(2,1)S(1)} collective-permute-done((bf16[256,1024]{1,0:T(8,128)(2,1)S(1)}, bf16[256,1024]{1,0:T(8,128)(2,1)S(1)}, u32[]{:S(2)}, u32[]{:S(2)}) %collective-permute-start.1) | collective-permute-done | bytes 524320 | tf_op jit(solution)/shard_map/ppermute | solution.py:14
  146.5 11.2 %collective-permute-start.3 = (bf16[256,1024]{1,0:T(8,128)(2,1)S(1)}, bf16[256,1024]{1,0:T(8,128)(2,1)S(1)}, u32[]{:S(2)}, u32[]{:S(2)}) collective-permute-start(bf16[256,1024]{1,0:T(8,128)(2,1)S(1)} %copy-done.25), channel_id=1, source_target_pairs={{0,1},{1,2},{2,3},{3,0},{4,5},{5,6},{6,7},{7,4},{8,9},{9,10},{10,1... | collective-permute-start | bytes 1572872 | tf_op jit(solution)/shard_map/ppermute | solution.py:14
  161.4 9.8 %collective-permute-done.3 = bf16[256,1024]{1,0:T(8,128)(2,1)S(1)} collective-permute-done((bf16[256,1024]{1,0:T(8,128)(2,1)S(1)}, bf16[256,1024]{1,0:T(8,128)(2,1)S(1)}, u32[]{:S(2)}, u32[]{:S(2)}) %collective-permute-start.3) | collective-permute-done | bytes 524320 | tf_op jit(solution)/shard_map/ppermute | solution.py:14
  171.3 21.3 %collective-permute-done.4 = bf16[256,1024]{1,0:T(8,128)(2,1)S(1)} collective-permute-done((bf16[256,1024]{1,0:T(8,128)(2,1)S(1)}, bf16[256,1024]{1,0:T(8,128)(2,1)S(1)}, u32[]{:S(2)}, u32[]{:S(2)}) %collective-permute-start.4) | collective-permute-done | bytes 524320 | tf_op jit(solution)/shard_map/ppermute | solution.py:14
  192.8 3.5 convolution_bitcast_fusion
  196.5 4.3 bitcast_dynamic-update-slice_fusion.11
  200.8 11.6 %collective-permute-start.17 = (bf16[256,1024]{1,0:T(8,128)(2,1)}, bf16[256,1024]{1,0:T(8,128)(2,1)S(1)}, u32[]{:S(2)}, u32[]{:S(2)}) collective-permute-start(bf16[256,1024]{1,0:T(8,128)(2,1)} %get-tuple-element.11), channel_id=1, source_target_pairs={{0,1},{1,2},{2,3},{3,0},{4,5},{5,6},{6,7},{7,4},{8,9},{9,10},{10,1... | collective-permute-start | bytes 1572872 | tf_op jit(solution)/shard_map/ppermute | solution.py:14
  215.4 3.5 convolution_bitcast_fusion.2
  218.8 4.3 multiply_reduce_fusion.7
  223.1 3.4 collective-permute-done.17
  226.6 20.7 %collective-permute-done.18 = bf16[256,1024]{1,0:T(8,128)(2,1)S(1)} collective-permute-done((bf16[256,1024]{1,0:T(8,128)(2,1)}, bf16[256,1024]{1,0:T(8,128)(2,1)S(1)}, u32[]{:S(2)}, u32[]{:S(2)}) %collective-permute-start.18) | collective-permute-done | bytes 524320 | tf_op jit(solution)/shard_map/ppermute | solution.py:14
  249.5 2.6 copy.36
  252.2 3.6 all-to-all-start.1
  261.1 13.5 %collective-permute-start.15 = (bf16[256,1024]{1,0:T(8,128)(2,1)}, bf16[256,1024]{1,0:T(8,128)(2,1)S(1)}, u32[]{:S(2)}, u32[]{:S(2)}) collective-permute-start(bf16[256,1024]{1,0:T(8,128)(2,1)} %get-tuple-element.45), channel_id=1, source_target_pairs={{0,3},{1,0},{2,1},{3,2},{4,7},{5,4},{6,5},{7,6},{8,11},{9,8},{10,9... | collective-permute-start | bytes 1572872 | tf_op jit(solution)/shard_map/ppermute | solution.py:14
  277.2 16.1 %collective-permute-done.20 = bf16[256,1024]{1,0:T(8,128)(2,1)S(1)} collective-permute-done((bf16[256,1024]{1,0:T(8,128)(2,1)}, bf16[256,1024]{1,0:T(8,128)(2,1)S(1)}, u32[]{:S(2)}, u32[]{:S(2)}) %collective-permute-start.20) | collective-permute-done | bytes 524320 | tf_op jit(solution)/shard_map/ppermute | solution.py:30
  293.2 11.5 %collective-permute-start.13 = (bf16[256,1024]{1,0:T(8,128)(2,1)S(1)}, bf16[256,1024]{1,0:T(8,128)(2,1)S(1)}, u32[]{:S(2)}, u32[]{:S(2)}) collective-permute-start(bf16[256,1024]{1,0:T(8,128)(2,1)S(1)} %copy-done.22), channel_id=1, source_target_pairs={{0,1},{1,2},{2,3},{3,0},{4,5},{5,6},{6,7},{7,4},{8,9},{9,10},{10,1... | collective-permute-start | bytes 1572872 | tf_op jit(solution)/shard_map/ppermute | solution.py:14
  308.8 10.5 %collective-permute-done.14 = bf16[256,1024]{1,0:T(8,128)(2,1)S(1)} collective-permute-done((bf16[256,1024]{1,0:T(8,128)(2,1)}, bf16[256,1024]{1,0:T(8,128)(2,1)S(1)}, u32[]{:S(2)}, u32[]{:S(2)}) %collective-permute-start.14) | collective-permute-done | bytes 524320 | tf_op jit(solution)/shard_map/ppermute | solution.py:14
  322.0 4.2 copy.31
  326.2 4.5 all-to-all-start
  336.4 4.1 copy.38
  340.5 3.9 fusion.21
  344.4 12.8 %all-to-all-done = bf16[4,256,1024]{1,0,2:T(4,128)(2,1)} async-done(((bf16[4,256,1024]{1,0,2:T(4,128)(2,1)}), bf16[4,256,1024]{1,0,2:T(4,128)(2,1)}, u32[]{:S(2)}, u32[]{:S(2)}) %all-to-all-start) | async-done | bytes 2097184 | tf_op jit(solution)/shard_map/all_to_all | solution.py:94
  359.1 2.4 copy.33
  361.5 3.3 fusion.25
  364.9 3.0 fusion.23
  367.9 4.6 fusion.53
  373.7 2.3 collective-permute-start.30
  378.6 20.2 %collective-permute-done.28 = bf16[4,128,1024]{2,1,0:T(8,128)(2,1)} collective-permute-done((bf16[4,128,1024]{2,1,0:T(8,128)(2,1)}, bf16[4,128,1024]{2,1,0:T(8,128)(2,1)}, u32[]{:S(2)}, u32[]{:S(2)}) %collective-permute-start.28) | collective-permute-done | bytes 1048608 | tf_op jit(solution)/shard_map/ppermute | solution.py:30
  400.5 20.1 %collective-permute-done.29 = bf16[4,128,1024]{2,1,0:T(8,128)(2,1)S(1)} collective-permute-done((bf16[4,128,1024]{2,1,0:T(8,128)(2,1)}, bf16[4,128,1024]{2,1,0:T(8,128)(2,1)S(1)}, u32[]{:S(2)}, u32[]{:S(2)}) %collective-permute-start.29) | collective-permute-done | bytes 1048608 | tf_op jit(solution)/shard_map/ppermute | solution.py:30
  423.1 2.3 copy.44
  428.7 6.2 %collective-permute-start.33 = (bf16[1024,512]{1,0:T(8,128)(2,1)S(1)}, bf16[1024,512]{1,0:T(8,128)(2,1)S(1)}, u32[]{:S(2)}, u32[]{:S(2)}) collective-permute-start(bf16[1024,512]{1,0:T(8,128)(2,1)S(1)} %convert_element_type.39), channel_id=1, source_target_pairs={{0,3},{1,0},{2,1},{3,2},{4,7},{5,4},{6,5},{7,6},{8,11},{9,8},{10,9... | collective-permute-start | bytes 3145736 | tf_op jit(solution)/shard_map/ppermute | solution.py:14
  438.5 20.0 %collective-permute-done.33 = bf16[1024,512]{1,0:T(8,128)(2,1)S(1)} collective-permute-done((bf16[1024,512]{1,0:T(8,128)(2,1)S(1)}, bf16[1024,512]{1,0:T(8,128)(2,1)S(1)}, u32[]{:S(2)}, u32[]{:S(2)}) %collective-permute-start.33) | collective-permute-done | bytes 1048608 | tf_op jit(solution)/shard_map/ppermute | solution.py:14
  459.4 65.9 %collective-permute-done.32 = bf16[1024,512]{1,0:T(8,128)(2,1)S(1)} collective-permute-done((bf16[1024,512]{1,0:T(8,128)(2,1)S(1)}, bf16[1024,512]{1,0:T(8,128)(2,1)S(1)}, u32[]{:S(2)}, u32[]{:S(2)}) %collective-permute-start.32) | collective-permute-done | bytes 1048608 | tf_op jit(solution)/shard_map/ppermute | solution.py:14
  527.1 39.4 %all-reduce = (f32[]{:T(128)}, f32[]{:T(128)}) all-reduce(f32[]{:T(128)} %get-tuple-element.18, f32[]{:T(128)} %get-tuple-element.23), channel_id=1, replica_groups=mesh['rows'=8,'cols'=4] {'rows','cols'}, use_global_device_ids=true, to_apply=%region_9.10 | all-reduce | flops 2 | bytes 16 | tf_op jit(solution)/shard_map/pmax | solution.py:105
  568.3 4.6 fusion
  572.9 5.9 %fusion.17 = f32[1024,512]{1,0:T(8,128)} fusion(f32[1024,512]{1,0:T(8,128)S(1)} %copy-done.8, f32[1024,512,1,1]{1,0,3,2:T(8,128)S(1)} %fusion, bf16[4,4,128,1024]{2,3,1,0:T(8,128)(2,1)} %collective-permute-done.34, bf16[4,1,128,512]{3,2,1,0:T(8,128)(2,1)S(1)} %get-tuple-element.30, bf16[4,1,128,512]{3,2,1,0:T(8,128)(2,1)S(1)} %get-tuple-element.28, ...), kind=kOutput, calls=%fused_computation.20 | convolution fusion | flops 2152202240 | bytes 12582916 | tf_op jit(solution)/shard_map/dot_general | solution.py:59
  (156 shorter events, 63.4 us)
Async XLA Ops:
  4.5 27.3 %collective-permute-start.6 = (bf16[1024,512]{1,0:T(8,128)(2,1)}, bf16[1024,512]{1,0:T(8,128)(2,1)}, u32[]{:S(2)}, u32[]{:S(2)}) collective-permute-start(bf16[1024,512]{1,0:T(8,128)(2,1)} %get-tuple-element.21), channel_id=1, source_target_pairs={{0,8},{4,12},{8,0},{12,4},{16,24},{20,28},{24,16},{28,20},{1,9},{5... | collective-permute-start | bytes 3145736 | tf_op jit(solution)/shard_map/ppermute | solution.py:30
  7.5 47.4 %collective-permute-start.7 = (bf16[1024,512]{1,0:T(8,128)(2,1)}, bf16[1024,512]{1,0:T(8,128)(2,1)}, u32[]{:S(2)}, u32[]{:S(2)}) collective-permute-start(bf16[1024,512]{1,0:T(8,128)(2,1)} %get-tuple-element.21), channel_id=1, source_target_pairs={{0,16},{4,20},{8,24},{12,28},{16,0},{20,4},{24,8},{28,12},{1,17},{... | collective-permute-start | bytes 3145736 | tf_op jit(solution)/shard_map/ppermute | solution.py:30
  9.1 48.1 %collective-permute-start.8 = (bf16[1024,512]{1,0:T(8,128)(2,1)}, bf16[1024,512]{1,0:T(8,128)(2,1)}, u32[]{:S(2)}, u32[]{:S(2)}) collective-permute-start(bf16[1024,512]{1,0:T(8,128)(2,1)} %get-tuple-element.21), channel_id=1, source_target_pairs={{0,24},{4,28},{8,16},{12,20},{16,8},{20,12},{24,0},{28,4},{1,25},{... | collective-permute-start | bytes 3145736 | tf_op jit(solution)/shard_map/ppermute | solution.py:30
  59.5 26.0 %collective-permute-start.9 = (bf16[1024,512]{1,0:T(8,128)(2,1)S(1)}, bf16[1024,512]{1,0:T(8,128)(2,1)S(1)}, u32[]{:S(2)}, u32[]{:S(2)}) collective-permute-start(bf16[1024,512]{1,0:T(8,128)(2,1)S(1)} %convert_element_type.39), channel_id=1, source_target_pairs={{0,8},{4,12},{8,0},{12,4},{16,24},{20,28},{24,16},{28,20},{1,9},{5... | collective-permute-start | bytes 3145736 | tf_op jit(solution)/shard_map/ppermute | solution.py:30
  59.5 45.3 %collective-permute-start.10 = (bf16[1024,512]{1,0:T(8,128)(2,1)S(1)}, bf16[1024,512]{1,0:T(8,128)(2,1)S(1)}, u32[]{:S(2)}, u32[]{:S(2)}) collective-permute-start(bf16[1024,512]{1,0:T(8,128)(2,1)S(1)} %convert_element_type.39), channel_id=1, source_target_pairs={{0,16},{4,20},{8,24},{12,28},{16,0},{20,4},{24,8},{28,12},{1,17},{... | collective-permute-start | bytes 3145736 | tf_op jit(solution)/shard_map/ppermute | solution.py:30
  61.5 45.2 %collective-permute-start.11 = (bf16[1024,512]{1,0:T(8,128)(2,1)S(1)}, bf16[1024,512]{1,0:T(8,128)(2,1)S(1)}, u32[]{:S(2)}, u32[]{:S(2)}) collective-permute-start(bf16[1024,512]{1,0:T(8,128)(2,1)S(1)} %convert_element_type.39), channel_id=1, source_target_pairs={{0,24},{4,28},{8,16},{12,20},{16,8},{20,12},{24,0},{28,4},{1,25},{... | collective-permute-start | bytes 3145736 | tf_op jit(solution)/shard_map/ppermute | solution.py:30
  63.0 129.8 %collective-permute-start.16 = (bf16[4,1024,512]{2,1,0:T(8,128)(2,1)}, bf16[4,1024,512]{2,1,0:T(8,128)(2,1)}, u32[]{:S(2)}, u32[]{:S(2)}) collective-permute-start(bf16[4,1024,512]{2,1,0:T(8,128)(2,1)} %bitcast_dynamic-update-slice_fusion.4), channel_id=1, source_target_pairs={{0,4},{4,0},{8,12},{12,8},{16,20},{20,16},{24,28},{28,24},{1,5},{5... | collective-permute-start | bytes 12582920 | tf_op jit(solution)/shard_map/ppermute | solution.py:32
  86.5 21.2 %copy-start.24 = (bf16[256,1024]{1,0:T(8,128)(2,1)S(1)}, bf16[256,1024]{1,0:T(8,128)(2,1)}, u32[]{:S(2)}) copy-start(bf16[256,1024]{1,0:T(8,128)(2,1)} %param.6) | copy-start | bytes 1572868
  107.7 38.8 %copy-start.25 = (bf16[256,1024]{1,0:T(8,128)(2,1)S(1)}, bf16[256,1024]{1,0:T(8,128)(2,1)}, u32[]{:S(2)}) copy-start(bf16[256,1024]{1,0:T(8,128)(2,1)} %param.5) | copy-start | bytes 1572868
  107.7 107.6 %collective-permute-start.12 = (bf16[4,1024,512]{2,1,0:T(8,128)(2,1)}, bf16[4,1024,512]{2,1,0:T(8,128)(2,1)}, u32[]{:S(2)}, u32[]{:S(2)}) collective-permute-start(bf16[4,1024,512]{2,1,0:T(8,128)(2,1)} %bitcast_dynamic-update-slice_fusion), channel_id=1, source_target_pairs={{0,4},{4,0},{8,12},{12,8},{16,20},{20,16},{24,28},{28,24},{1,5},{5... | collective-permute-start | bytes 12582920 | tf_op jit(solution)/shard_map/ppermute | solution.py:32
  107.7 16.9 %collective-permute-start = (bf16[256,1024]{1,0:T(8,128)(2,1)S(1)}, bf16[256,1024]{1,0:T(8,128)(2,1)}, u32[]{:S(2)}, u32[]{:S(2)}) collective-permute-start(bf16[256,1024]{1,0:T(8,128)(2,1)S(1)} %copy-done.24), channel_id=1, source_target_pairs={{0,1},{1,2},{2,3},{3,0},{4,5},{5,6},{6,7},{7,4},{8,9},{9,10},{10,1... | collective-permute-start | bytes 1572872 | tf_op jit(solution)/shard_map/ppermute | solution.py:14
  108.4 38.0 %collective-permute-start.1 = (bf16[256,1024]{1,0:T(8,128)(2,1)S(1)}, bf16[256,1024]{1,0:T(8,128)(2,1)S(1)}, u32[]{:S(2)}, u32[]{:S(2)}) collective-permute-start(bf16[256,1024]{1,0:T(8,128)(2,1)S(1)} %copy-done.24), channel_id=1, source_target_pairs={{0,2},{1,3},{2,0},{3,1},{4,6},{5,7},{6,4},{7,5},{8,10},{9,11},{10,... | collective-permute-start | bytes 1572872 | tf_op jit(solution)/shard_map/ppermute | solution.py:14
  111.0 35.4 %collective-permute-start.2 = (bf16[256,1024]{1,0:T(8,128)(2,1)S(1)}, bf16[256,1024]{1,0:T(8,128)(2,1)S(1)}, u32[]{:S(2)}, u32[]{:S(2)}) collective-permute-start(bf16[256,1024]{1,0:T(8,128)(2,1)S(1)} %copy-done.24), channel_id=1, source_target_pairs={{0,3},{1,0},{2,1},{3,2},{4,7},{5,4},{6,5},{7,6},{8,11},{9,8},{10,9... | collective-permute-start | bytes 1572872 | tf_op jit(solution)/shard_map/ppermute | solution.py:14
  146.5 24.8 %collective-permute-start.3 = (bf16[256,1024]{1,0:T(8,128)(2,1)S(1)}, bf16[256,1024]{1,0:T(8,128)(2,1)S(1)}, u32[]{:S(2)}, u32[]{:S(2)}) collective-permute-start(bf16[256,1024]{1,0:T(8,128)(2,1)S(1)} %copy-done.25), channel_id=1, source_target_pairs={{0,1},{1,2},{2,3},{3,0},{4,5},{5,6},{6,7},{7,4},{8,9},{9,10},{10,1... | collective-permute-start | bytes 1572872 | tf_op jit(solution)/shard_map/ppermute | solution.py:14
  157.7 35.0 %collective-permute-start.4 = (bf16[256,1024]{1,0:T(8,128)(2,1)S(1)}, bf16[256,1024]{1,0:T(8,128)(2,1)S(1)}, u32[]{:S(2)}, u32[]{:S(2)}) collective-permute-start(bf16[256,1024]{1,0:T(8,128)(2,1)S(1)} %copy-done.25), channel_id=1, source_target_pairs={{0,2},{1,3},{2,0},{3,1},{4,6},{5,7},{6,4},{7,5},{8,10},{9,11},{10,... | collective-permute-start | bytes 1572872 | tf_op jit(solution)/shard_map/ppermute | solution.py:14
  158.9 33.8 %collective-permute-start.5 = (bf16[256,1024]{1,0:T(8,128)(2,1)S(1)}, bf16[256,1024]{1,0:T(8,128)(2,1)S(1)}, u32[]{:S(2)}, u32[]{:S(2)}) collective-permute-start(bf16[256,1024]{1,0:T(8,128)(2,1)S(1)} %copy-done.25), channel_id=1, source_target_pairs={{0,3},{1,0},{2,1},{3,2},{4,7},{5,4},{6,5},{7,6},{8,11},{9,8},{10,9... | collective-permute-start | bytes 1572872 | tf_op jit(solution)/shard_map/ppermute | solution.py:14
  200.8 18.1 %copy-start = (bf16[4,256,1024]{2,1,0:T(8,128)(2,1)}, bf16[4,256,1024]{2,1,0:T(8,128)(2,1)S(1)}, u32[]{:S(2)}) copy-start(bf16[4,256,1024]{2,1,0:T(8,128)(2,1)S(1)} %get-tuple-element.46) | copy-start | bytes 6291460
  200.8 25.8 %collective-permute-start.17 = (bf16[256,1024]{1,0:T(8,128)(2,1)}, bf16[256,1024]{1,0:T(8,128)(2,1)S(1)}, u32[]{:S(2)}, u32[]{:S(2)}) collective-permute-start(bf16[256,1024]{1,0:T(8,128)(2,1)} %get-tuple-element.11), channel_id=1, source_target_pairs={{0,1},{1,2},{2,3},{3,0},{4,5},{5,6},{6,7},{7,4},{8,9},{9,10},{10,1... | collective-permute-start | bytes 1572872 | tf_op jit(solution)/shard_map/ppermute | solution.py:14
  212.4 34.8 %collective-permute-start.18 = (bf16[256,1024]{1,0:T(8,128)(2,1)}, bf16[256,1024]{1,0:T(8,128)(2,1)S(1)}, u32[]{:S(2)}, u32[]{:S(2)}) collective-permute-start(bf16[256,1024]{1,0:T(8,128)(2,1)} %get-tuple-element.11), channel_id=1, source_target_pairs={{0,2},{1,3},{2,0},{3,1},{4,6},{5,7},{6,4},{7,5},{8,10},{9,11},{10,... | collective-permute-start | bytes 1572872 | tf_op jit(solution)/shard_map/ppermute | solution.py:14
  214.0 33.3 %collective-permute-start.19 = (bf16[256,1024]{1,0:T(8,128)(2,1)}, bf16[256,1024]{1,0:T(8,128)(2,1)S(1)}, u32[]{:S(2)}, u32[]{:S(2)}) collective-permute-start(bf16[256,1024]{1,0:T(8,128)(2,1)} %get-tuple-element.11), channel_id=1, source_target_pairs={{0,3},{1,0},{2,1},{3,2},{4,7},{5,4},{6,5},{7,6},{8,11},{9,8},{10,9... | collective-permute-start | bytes 1572872 | tf_op jit(solution)/shard_map/ppermute | solution.py:14
  214.8 44.4 %collective-permute-start.24 = (bf16[256,1024]{1,0:T(8,128)(2,1)}, bf16[256,1024]{1,0:T(8,128)(2,1)}, u32[]{:S(2)}, u32[]{:S(2)}) collective-permute-start(bf16[256,1024]{1,0:T(8,128)(2,1)} %get-tuple-element.11), channel_id=1, source_target_pairs={{0,8},{4,12},{8,0},{12,4},{16,24},{20,28},{24,16},{28,20},{1,9},{5... | collective-permute-start | bytes 1572872 | tf_op jit(solution)/shard_map/ppermute | solution.py:30
  226.6 20.7 %copy-start.10 = (bf16[256,1024]{1,0:T(8,128)(2,1)}, bf16[256,1024]{1,0:T(8,128)(2,1)S(1)}, u32[]{:S(2)}) copy-start(bf16[256,1024]{1,0:T(8,128)(2,1)S(1)} %collective-permute-done.17) | copy-start | bytes 1572868
  252.2 74.0 %all-to-all-start.1 = ((bf16[4,256,1024]{1,0,2:T(4,128)(2,1)}), bf16[4,256,1024]{1,0,2:T(4,128)(2,1)S(1)}, u32[]{:S(2)}, u32[]{:S(2)}) async-start(bf16[4,256,1024]{1,0,2:T(4,128)(2,1)} %copy.36), calls=%async_computation.1 | async-start | bytes 4194304 | tf_op jit(solution)/shard_map/all_to_all | solution.py:94
  255.8 20.6 %copy-start.22 = (bf16[256,1024]{1,0:T(8,128)(2,1)S(1)}, bf16[256,1024]{1,0:T(8,128)(2,1)}, u32[]{:S(2)}) copy-start(bf16[256,1024]{1,0:T(8,128)(2,1)} %get-tuple-element.45) | copy-start | bytes 1572868
  255.8 37.5 %collective-permute-start.20 = (bf16[256,1024]{1,0:T(8,128)(2,1)}, bf16[256,1024]{1,0:T(8,128)(2,1)S(1)}, u32[]{:S(2)}, u32[]{:S(2)}) collective-permute-start(bf16[256,1024]{1,0:T(8,128)(2,1)} %get-tuple-element.45), channel_id=1, source_target_pairs={{0,8},{4,12},{8,0},{12,4},{16,24},{20,28},{24,16},{28,20},{1,9},{5... | collective-permute-start | bytes 1572872 | tf_op jit(solution)/shard_map/ppermute | solution.py:30
  257.7 47.9 %collective-permute-start.21 = (bf16[256,1024]{1,0:T(8,128)(2,1)}, bf16[256,1024]{1,0:T(8,128)(2,1)S(1)}, u32[]{:S(2)}, u32[]{:S(2)}) collective-permute-start(bf16[256,1024]{1,0:T(8,128)(2,1)} %get-tuple-element.45), channel_id=1, source_target_pairs={{0,16},{4,20},{8,24},{12,28},{16,0},{20,4},{24,8},{28,12},{1,17},{... | collective-permute-start | bytes 1572872 | tf_op jit(solution)/shard_map/ppermute | solution.py:30
  261.1 47.7 %collective-permute-start.15 = (bf16[256,1024]{1,0:T(8,128)(2,1)}, bf16[256,1024]{1,0:T(8,128)(2,1)S(1)}, u32[]{:S(2)}, u32[]{:S(2)}) collective-permute-start(bf16[256,1024]{1,0:T(8,128)(2,1)} %get-tuple-element.45), channel_id=1, source_target_pairs={{0,3},{1,0},{2,1},{3,2},{4,7},{5,4},{6,5},{7,6},{8,11},{9,8},{10,9... | collective-permute-start | bytes 1572872 | tf_op jit(solution)/shard_map/ppermute | solution.py:14
  274.6 44.7 %collective-permute-start.14 = (bf16[256,1024]{1,0:T(8,128)(2,1)}, bf16[256,1024]{1,0:T(8,128)(2,1)S(1)}, u32[]{:S(2)}, u32[]{:S(2)}) collective-permute-start(bf16[256,1024]{1,0:T(8,128)(2,1)} %get-tuple-element.45), channel_id=1, source_target_pairs={{0,2},{1,3},{2,0},{3,1},{4,6},{5,7},{6,4},{7,5},{8,10},{9,11},{10,... | collective-permute-start | bytes 1572872 | tf_op jit(solution)/shard_map/ppermute | solution.py:14
  274.6 33.3 %collective-permute-start.22 = (bf16[256,1024]{1,0:T(8,128)(2,1)}, bf16[256,1024]{1,0:T(8,128)(2,1)S(1)}, u32[]{:S(2)}, u32[]{:S(2)}) collective-permute-start(bf16[256,1024]{1,0:T(8,128)(2,1)} %get-tuple-element.45), channel_id=1, source_target_pairs={{0,24},{4,28},{8,16},{12,20},{16,8},{20,12},{24,0},{28,4},{1,25},{... | collective-permute-start | bytes 1572872 | tf_op jit(solution)/shard_map/ppermute | solution.py:30
  293.2 26.1 %collective-permute-start.13 = (bf16[256,1024]{1,0:T(8,128)(2,1)S(1)}, bf16[256,1024]{1,0:T(8,128)(2,1)S(1)}, u32[]{:S(2)}, u32[]{:S(2)}) collective-permute-start(bf16[256,1024]{1,0:T(8,128)(2,1)S(1)} %copy-done.22), channel_id=1, source_target_pairs={{0,1},{1,2},{2,3},{3,0},{4,5},{5,6},{6,7},{7,4},{8,9},{9,10},{10,1... | collective-permute-start | bytes 1572872 | tf_op jit(solution)/shard_map/ppermute | solution.py:14
  305.6 25.2 %collective-permute-start.25 = (bf16[256,1024]{1,0:T(8,128)(2,1)}, bf16[256,1024]{1,0:T(8,128)(2,1)}, u32[]{:S(2)}, u32[]{:S(2)}) collective-permute-start(bf16[256,1024]{1,0:T(8,128)(2,1)} %get-tuple-element.11), channel_id=1, source_target_pairs={{0,16},{4,20},{8,24},{12,28},{16,0},{20,4},{24,8},{28,12},{1,17},{... | collective-permute-start | bytes 1572872 | tf_op jit(solution)/shard_map/ppermute | solution.py:30
  307.9 24.7 %collective-permute-start.26 = (bf16[256,1024]{1,0:T(8,128)(2,1)}, bf16[256,1024]{1,0:T(8,128)(2,1)}, u32[]{:S(2)}, u32[]{:S(2)}) collective-permute-start(bf16[256,1024]{1,0:T(8,128)(2,1)} %get-tuple-element.11), channel_id=1, source_target_pairs={{0,24},{4,28},{8,16},{12,20},{16,8},{20,12},{24,0},{28,4},{1,25},{... | collective-permute-start | bytes 1572872 | tf_op jit(solution)/shard_map/ppermute | solution.py:30
  308.8 10.5 %copy-start.16 = (bf16[256,1024]{1,0:T(8,128)(2,1)}, bf16[256,1024]{1,0:T(8,128)(2,1)S(1)}, u32[]{:S(2)}) copy-start(bf16[256,1024]{1,0:T(8,128)(2,1)S(1)} %collective-permute-done.15) | copy-start | bytes 1572868
  308.8 56.0 %collective-permute-start.23 = (bf16[4,256,1024]{2,1,0:T(8,128)(2,1)}, bf16[4,256,1024]{2,1,0:T(8,128)(2,1)}, u32[]{:S(2)}, u32[]{:S(2)}) collective-permute-start(bf16[4,256,1024]{2,1,0:T(8,128)(2,1)} %bitcast_dynamic-update-slice_fusion.12), channel_id=1, source_target_pairs={{0,4},{4,0},{8,12},{12,8},{16,20},{20,16},{24,28},{28,24},{1,5},{5... | collective-permute-start | bytes 6291464 | tf_op jit(solution)/shard_map/ppermute | solution.py:32
  326.2 31.0 %all-to-all-start = ((bf16[4,256,1024]{1,0,2:T(4,128)(2,1)}), bf16[4,256,1024]{1,0,2:T(4,128)(2,1)}, u32[]{:S(2)}, u32[]{:S(2)}) async-start(bf16[4,256,1024]{1,0,2:T(4,128)(2,1)} %copy.31), calls=%async_computation | async-start | bytes 4194304 | tf_op jit(solution)/shard_map/all_to_all | solution.py:94
  334.5 33.4 %collective-permute-start.27 = (bf16[4,256,1024]{2,1,0:T(8,128)(2,1)}, bf16[4,256,1024]{2,1,0:T(8,128)(2,1)}, u32[]{:S(2)}, u32[]{:S(2)}) collective-permute-start(bf16[4,256,1024]{2,1,0:T(8,128)(2,1)} %bitcast_dynamic-update-slice_fusion.8), channel_id=1, source_target_pairs={{0,4},{4,0},{8,12},{12,8},{16,20},{20,16},{24,28},{28,24},{1,5},{5... | collective-permute-start | bytes 6291464 | tf_op jit(solution)/shard_map/ppermute | solution.py:32
  372.5 26.3 %collective-permute-start.28 = (bf16[4,128,1024]{2,1,0:T(8,128)(2,1)}, bf16[4,128,1024]{2,1,0:T(8,128)(2,1)}, u32[]{:S(2)}, u32[]{:S(2)}) collective-permute-start(bf16[4,128,1024]{2,1,0:T(8,128)(2,1)} %get-tuple-element.22), channel_id=1, source_target_pairs={{0,8},{4,12},{8,0},{12,4},{16,24},{20,28},{24,16},{28,20},{1,9},{5... | collective-permute-start | bytes 3145736 | tf_op jit(solution)/shard_map/ppermute | solution.py:30
  373.0 47.5 %collective-permute-start.29 = (bf16[4,128,1024]{2,1,0:T(8,128)(2,1)}, bf16[4,128,1024]{2,1,0:T(8,128)(2,1)S(1)}, u32[]{:S(2)}, u32[]{:S(2)}) collective-permute-start(bf16[4,128,1024]{2,1,0:T(8,128)(2,1)} %get-tuple-element.22), channel_id=1, source_target_pairs={{0,16},{4,20},{8,24},{12,28},{16,0},{20,4},{24,8},{28,12},{1,17},{... | collective-permute-start | bytes 3145736 | tf_op jit(solution)/shard_map/ppermute | solution.py:30
  373.7 49.5 %collective-permute-start.30 = (bf16[4,128,1024]{2,1,0:T(8,128)(2,1)}, bf16[4,128,1024]{2,1,0:T(8,128)(2,1)}, u32[]{:S(2)}, u32[]{:S(2)}) collective-permute-start(bf16[4,128,1024]{2,1,0:T(8,128)(2,1)} %get-tuple-element.22), channel_id=1, source_target_pairs={{0,24},{4,28},{8,16},{12,20},{16,8},{20,12},{24,0},{28,4},{1,25},{... | collective-permute-start | bytes 3145736 | tf_op jit(solution)/shard_map/ppermute | solution.py:30
  378.6 20.2 %copy-start.6 = (bf16[4,4,128,1024]{2,3,1,0:T(8,128)(2,1)}, bf16[4,4,128,1024]{2,3,1,0:T(8,128)(2,1)S(1)}, u32[]{:S(2)}) copy-start(bf16[4,4,128,1024]{2,3,1,0:T(8,128)(2,1)S(1)} %constant_dynamic-update-slice_fusion.4) | copy-start | bytes 12582916
  426.5 8.4 %copy-start.13 = (bf16[256,1024]{1,0:T(8,128)(2,1)S(1)}, bf16[256,1024]{1,0:T(8,128)(2,1)}, u32[]{:S(2)}) copy-start(bf16[256,1024]{1,0:T(8,128)(2,1)} %copy-done.12) | copy-start | bytes 1572868
  426.5 8.4 %copy-start.15 = (bf16[256,1024]{1,0:T(8,128)(2,1)S(1)}, bf16[256,1024]{1,0:T(8,128)(2,1)}, u32[]{:S(2)}) copy-start(bf16[256,1024]{1,0:T(8,128)(2,1)} %copy-done.14) | copy-start | bytes 1572868
  428.6 8.7 %copy-start.17 = (bf16[256,1024]{1,0:T(8,128)(2,1)S(1)}, bf16[256,1024]{1,0:T(8,128)(2,1)}, u32[]{:S(2)}) copy-start(bf16[256,1024]{1,0:T(8,128)(2,1)} %copy-done.16) | copy-start | bytes 1572868
  428.7 144.2 %collective-permute-start.34 = (bf16[4,4,128,1024]{2,3,1,0:T(8,128)(2,1)}, bf16[4,4,128,1024]{2,3,1,0:T(8,128)(2,1)}, u32[]{:S(2)}, u32[]{:S(2)}) collective-permute-start(bf16[4,4,128,1024]{2,3,1,0:T(8,128)(2,1)} %constant_dynamic-update-slice_fusion.1), channel_id=1, source_target_pairs={{0,4},{4,0},{8,12},{12,8},{16,20},{20,16},{24,28},{28,24},{1,5},{5... | collective-permute-start | bytes 12582920 | tf_op jit(solution)/shard_map/ppermute | solution.py:32
  428.7 29.9 %collective-permute-start.33 = (bf16[1024,512]{1,0:T(8,128)(2,1)S(1)}, bf16[1024,512]{1,0:T(8,128)(2,1)S(1)}, u32[]{:S(2)}, u32[]{:S(2)}) collective-permute-start(bf16[1024,512]{1,0:T(8,128)(2,1)S(1)} %convert_element_type.39), channel_id=1, source_target_pairs={{0,3},{1,0},{2,1},{3,2},{4,7},{5,4},{6,5},{7,6},{8,11},{9,8},{10,9... | collective-permute-start | bytes 3145736 | tf_op jit(solution)/shard_map/ppermute | solution.py:14
  435.2 90.1 %collective-permute-start.32 = (bf16[1024,512]{1,0:T(8,128)(2,1)S(1)}, bf16[1024,512]{1,0:T(8,128)(2,1)S(1)}, u32[]{:S(2)}, u32[]{:S(2)}) collective-permute-start(bf16[1024,512]{1,0:T(8,128)(2,1)S(1)} %convert_element_type.39), channel_id=1, source_target_pairs={{0,2},{1,3},{2,0},{3,1},{4,6},{5,7},{6,4},{7,5},{8,10},{9,11},{10,... | collective-permute-start | bytes 3145736 | tf_op jit(solution)/shard_map/ppermute | solution.py:14
  436.7 89.5 %collective-permute-start.31 = (bf16[1024,512]{1,0:T(8,128)(2,1)S(1)}, bf16[1024,512]{1,0:T(8,128)(2,1)S(1)}, u32[]{:S(2)}, u32[]{:S(2)}) collective-permute-start(bf16[1024,512]{1,0:T(8,128)(2,1)S(1)} %convert_element_type.39), channel_id=1, source_target_pairs={{0,1},{1,2},{2,3},{3,0},{4,5},{5,6},{6,7},{7,4},{8,9},{9,10},{10,1... | collective-permute-start | bytes 3145736 | tf_op jit(solution)/shard_map/ppermute | solution.py:14
  526.2 42.1 %copy-start.26 = (bf16[4,1,128,512]{3,2,1,0:T(8,128)(2,1)S(1)}, bf16[4,1,128,512]{3,2,1,0:T(8,128)(2,1)}, u32[]{:S(2)}) copy-start(bf16[4,1,128,512]{3,2,1,0:T(8,128)(2,1)} %get-tuple-element.29) | copy-start | bytes 1572868
  (17 other events, 50.8 us)
